TPU v7x, 512 devices: a whole 4x4x16 slice. The times are simulated.
512 devices in a mesh: gx: 16 (over z), gz: 32 (over x, y, core).
Axes of the slice: x: 4, y: 4, z: 16, core: 2. Of those that a mesh axis runs over, the one named last changes fastest.
Arguments:
- velocity: float32 [3, 4096, 1, 4096], P(None, 'gx', None, 'gz'), may hold values from -6 to 6
Outputs:
- advection: float32 [3, 4096, 1, 4096], P(None, 'gx', None, 'gz')
All inputs are finite; a program needn't handle non-finite values.
Results may differ from a plain program's by a relative error of at most 0.00013.
Values sent between devices are 32-bit elements; how exact they have to be, the bound alone decides.
A program may use at most 64 MiB of HBM per device.

v0:
```python
import jax
import jax.numpy as jnp
from jax import lax
from jax.sharding import PartitionSpec as P

ALPHA_D = 1.0 / 3.0
COEF_A = 14.0 / 9.0
COEF_B = 1.0 / 9.0
ALPHA_F = 0.49
block_len = 128


def with_halo(block, sides, width):
    for axis, dim in sides:
        count = lax.axis_size(axis)
        forward = [(i, i + 1) for i in range(count - 1)]
        forward.append((count - 1, 0))
        backward = [(target, source) for source, target in forward]
        low = lax.ppermute(
            lax.slice_in_dim(block, block.shape[dim] - width, None, axis=dim), axis, forward
        )
        high = lax.ppermute(lax.slice_in_dim(block, 0, width, axis=dim), axis, backward)
        block = jnp.concatenate([low, block, high], axis=dim)
    return block


def filter_coefficients():
    return (
        (11.0 + 10.0 * ALPHA_F) / 16.0,
        (15.0 + 34.0 * ALPHA_F) / 32.0,
        (-3.0 + 6.0 * ALPHA_F) / 16.0,
        (1.0 - 2.0 * ALPHA_F) / 32.0,
    )


def tables(length, alpha):
    lower_diag = jnp.concatenate(
        [jnp.zeros((1,), jnp.float32), jnp.full((length - 1,), alpha, jnp.float32)]
    )
    upper_diag = jnp.concatenate(
        [jnp.full((length - 1,), alpha, jnp.float32), jnp.zeros((1,), jnp.float32)]
    )
    main_diag = jnp.ones((length,), jnp.float32)
    identity = jnp.eye(length, dtype=jnp.float32)
    inverse = lax.linalg.tridiagonal_solve(lower_diag, main_diag, upper_diag, identity)
    left_col = alpha * inverse[:, 0]
    right_col = alpha * inverse[:, length - 1]
    coupling = alpha * inverse[0, 0]
    return (inverse, left_col, right_col, coupling)


def offset_slice(extended, offset, length, direction, base=3):
    return lax.slice_in_dim(extended, base + offset, base + offset + length, axis=direction)


def slope_rhs(extended, length, direction, base=3):
    rhs = (
        COEF_A
        * 0.5
        * (
            offset_slice(extended, 1, length, direction, base)
            - offset_slice(extended, -1, length, direction, base)
        )
    )
    return rhs + COEF_B * 0.25 * (
        offset_slice(extended, 2, length, direction, base)
        - offset_slice(extended, -2, length, direction, base)
    )


def smooth_rhs(extended, length, direction, base=3):
    coefficients = filter_coefficients()
    rhs = coefficients[0] * offset_slice(extended, 0, length, direction, base)
    for offset in range(1, 4):
        rhs = rhs + 0.5 * coefficients[offset] * (
            offset_slice(extended, offset, length, direction, base)
            + offset_slice(extended, -offset, length, direction, base)
        )
    return rhs


def wrap_pad(values, direction):
    length = values.shape[direction]
    return jnp.concatenate(
        [
            lax.slice_in_dim(values, length - 3, length, axis=direction),
            values,
            lax.slice_in_dim(values, 0, 3, axis=direction),
        ],
        axis=direction,
    )


def apply_along(inverse, values, direction):
    rotated = jnp.tensordot(
        inverse, values, axes=([1], [direction]), precision=lax.Precision.HIGHEST
    )
    return jnp.moveaxis(rotated, 0, direction)


def end_values(partial_value, direction):
    length = partial_value.shape[direction]
    first_val = lax.slice_in_dim(partial_value, 0, 1, axis=direction)
    last_val = lax.slice_in_dim(partial_value, length - 1, length, axis=direction)
    return (first_val, last_val)


def corrected(partial_value, prev_last, next_first, table, direction):
    inverse, left_col, right_col, coupling = table
    first_val, last_val = end_values(partial_value, direction)
    factor_inv = 1.0 / (1.0 - coupling * coupling)
    left_value = (prev_last - coupling * first_val) * factor_inv
    right_value = (next_first - coupling * last_val) * factor_inv
    dims_list = [1] * partial_value.ndim
    dims_list[direction] = partial_value.shape[direction]
    return (
        partial_value
        - left_col.reshape(dims_list) * left_value
        - right_col.reshape(dims_list) * right_value
    )


def extend_x(values):
    return with_halo(values, (("gx", 1),), 3)


def solve_x(rhs, table):
    partial_value = apply_along(table[0], rhs, 1)
    first_val, last_val = end_values(partial_value, 1)
    beside = with_halo(jnp.concatenate([first_val, last_val], axis=1), (("gx", 1),), 1)
    return corrected(partial_value, beside[:, 0:1], beside[:, 3:4], table, 1)


def solve_blocks(rhs, table):
    dims_list = rhs.shape
    blocks = rhs.reshape(dims_list[:-1] + (dims_list[-1] // block_len, block_len))
    last_dim = blocks.ndim - 1
    partial_value = apply_along(table[0], blocks, last_dim)
    first_val, last_val = end_values(partial_value, last_dim)
    prev_last = jnp.roll(last_val, 1, axis=last_dim - 1)
    next_first = jnp.roll(first_val, -1, axis=last_dim - 1)
    return corrected(partial_value, prev_last, next_first, table, last_dim).reshape(dims_list)


def z_part(velocity):
    slope_z = tables(block_len, ALPHA_D)
    pencil = lax.all_to_all(velocity, "gz", split_axis=1, concat_axis=3, tiled=True)
    along_z = pencil[2:3]
    fields = jnp.concatenate([pencil, along_z * pencil], axis=0)
    slopes = solve_blocks(slope_rhs(wrap_pad(fields, 3), fields.shape[3], 3), slope_z)
    local_terms = slopes[3:] + along_z * slopes[:3]
    return lax.all_to_all(local_terms, "gz", split_axis=3, concat_axis=1, tiled=True)


def per_device(velocity):
    width_x = velocity.shape[1]
    slope_x = tables(width_x, ALPHA_D)
    smooth_x = tables(width_x, ALPHA_F)
    along_x = velocity[0:1]
    rim_source = jnp.concatenate([velocity, along_x * velocity], axis=0)
    padded = extend_x(rim_source)
    slopes_x = solve_x(slope_rhs(padded, width_x, 1), slope_x)
    x_terms = slopes_x[3:] + along_x * slopes_x[:3]
    z_terms = z_part(velocity)
    combined = 0.5 * (x_terms + z_terms)
    smoothed = solve_x(smooth_rhs(extend_x(combined), width_x, 1), smooth_x)
    return -smoothed


def solution(mesh):
    return jax.shard_map(
        per_device,
        mesh=mesh,
        in_specs=(P(None, "gx", None, "gz"),),
        out_specs=P(None, "gx", None, "gz"),
        check_vma=False,
    )
```

profile of v0, /device:TPU:2, one launch (start us, length us, event | category | flops | bytes accessed | tf_op | source)
XLA Modules:
  0.0 653.2 jit_solution(18233440407456017549)
XLA Ops:
  33.8 14.9 %while.98 = (s32[]{:T(128)}, f32[]{:T(128)}, f32[256]{0:T(256)S(1)}, f32[7,32]{1,0:T(8,128)S(1)}, f32[7,32,256]{2,1,0:T(8,128)S(1)}, /*index=5*/f32[7,32,256]{2,...) while((s32[]{:T(128)}, f32[]{:T(128)}, ...), condition=%wide.region_5.6_spmd, body=%wide.region_4.5_spmd.sunk | while | flops 24705 | bytes 267885 | solution.py:45
  68.5 64.5 %while.101 = (s32[]{:T(128)}, f32[128]{0:T(128)S(1)}, f32[3,32,128]{2,1,0:T(8,128)S(1)}, f32[3,32,128]{2,1,0:T(8,128)S(1)}, f32[3,32]{1,0:T(4,128)S(1)}, /*index...) while((s32[]{:T(128)}, f32[128]{0:T(128)S(1)}, ...), condition=%wide.region_11.12_spmd, body=%wide.region_10.11_spmd.sunk | while | flops 8226 | bytes 101341 | solution.py:45
  69.9 19.9 %fusion.491 = (f32[128]{0:T(128)S(1)}, f32[128]{0:T(128)S(1)}, f32[128]{0:T(128)S(1)}, f32[128]{0:T(128)S(1)}, f32[128]{0:T(128)S(1)}, /*index=5*/f32[128]{0:T(1...) fusion(f32[3,32,128]{2,1,0:T(8,128)S(1)} %get-tuple-element.256, ...), kind=kLoop, calls=%fused_computation.428.clone.1 | loop fusion | flops 8192 | bytes 33536 | tf_op jit(solution)/shard_map/while/body/eval_jaxpr/sub | solution.py:45
  91.4 19.9 %fusion.491 = (f32[128]{0:T(128)S(1)}, f32[128]{0:T(128)S(1)}, f32[128]{0:T(128)S(1)}, f32[128]{0:T(128)S(1)}, f32[128]{0:T(128)S(1)}, /*index=5*/f32[128]{0:T(1...) fusion(f32[3,32,128]{2,1,0:T(8,128)S(1)} %get-tuple-element.256, ...), kind=kLoop, calls=%fused_computation.428.clone.1 | loop fusion | flops 8192 | bytes 33536 | tf_op jit(solution)/shard_map/while/body/eval_jaxpr/sub | solution.py:45
  112.9 19.9 %fusion.491 = (f32[128]{0:T(128)S(1)}, f32[128]{0:T(128)S(1)}, f32[128]{0:T(128)S(1)}, f32[128]{0:T(128)S(1)}, f32[128]{0:T(128)S(1)}, /*index=5*/f32[128]{0:T(1...) fusion(f32[3,32,128]{2,1,0:T(8,128)S(1)} %get-tuple-element.256, ...), kind=kLoop, calls=%fused_computation.428.clone.1 | loop fusion | flops 8192 | bytes 33536 | tf_op jit(solution)/shard_map/while/body/eval_jaxpr/sub | solution.py:45
  175.7 153.7 %while.99 = (s32[]{:T(128)}, f32[256]{0:T(256)S(1)}, f32[7,32,256]{2,1,0:T(8,128)S(1)}, f32[7,32,256]{2,1,0:T(8,128)S(1)}, f32[7,32]{1,0:T(8,128)S(1)}, /*index=...) while((s32[]{:T(128)}, f32[256]{0:T(256)S(1)}, ...), condition=%wide.region_7.8_spmd, body=%wide.region_6.7_spmd.sunk | while | flops 16418 | bytes 266721 | solution.py:45
  177.4 20.2 %multiply_subtract_fusion.253 = (f32[256]{0:T(256)S(1)}, f32[256]{0:T(256)S(1)}, f32[256]{0:T(256)S(1)}, f32[256]{0:T(256)S(1)}, f32[256]{0:T(256)S(1)}, /*index...) fusion(f32[256]{0:T(256)S(1)} %bitcast.3158, ...), kind=kLoop, calls=%fused_computation.230.clone.1 | loop fusion | flops 16384 | bytes 66688 | tf_op jit(solution)/shard_map/while/body/eval_jaxpr/sub | solution.py:45
  199.4 20.2 %multiply_subtract_fusion.253 = (f32[256]{0:T(256)S(1)}, f32[256]{0:T(256)S(1)}, f32[256]{0:T(256)S(1)}, f32[256]{0:T(256)S(1)}, f32[256]{0:T(256)S(1)}, /*index...) fusion(f32[256]{0:T(256)S(1)} %bitcast.3158, ...), kind=kLoop, calls=%fused_computation.230.clone.1 | loop fusion | flops 16384 | bytes 66688 | tf_op jit(solution)/shard_map/while/body/eval_jaxpr/sub | solution.py:45
  221.3 20.2 %multiply_subtract_fusion.253 = (f32[256]{0:T(256)S(1)}, f32[256]{0:T(256)S(1)}, f32[256]{0:T(256)S(1)}, f32[256]{0:T(256)S(1)}, f32[256]{0:T(256)S(1)}, /*index...) fusion(f32[256]{0:T(256)S(1)} %bitcast.3158, ...), kind=kLoop, calls=%fused_computation.230.clone.1 | loop fusion | flops 16384 | bytes 66688 | tf_op jit(solution)/shard_map/while/body/eval_jaxpr/sub | solution.py:45
  243.3 20.2 %multiply_subtract_fusion.253 = (f32[256]{0:T(256)S(1)}, f32[256]{0:T(256)S(1)}, f32[256]{0:T(256)S(1)}, f32[256]{0:T(256)S(1)}, f32[256]{0:T(256)S(1)}, /*index...) fusion(f32[256]{0:T(256)S(1)} %bitcast.3158, ...), kind=kLoop, calls=%fused_computation.230.clone.1 | loop fusion | flops 16384 | bytes 66688 | tf_op jit(solution)/shard_map/while/body/eval_jaxpr/sub | solution.py:45
  265.2 20.2 %multiply_subtract_fusion.253 = (f32[256]{0:T(256)S(1)}, f32[256]{0:T(256)S(1)}, f32[256]{0:T(256)S(1)}, f32[256]{0:T(256)S(1)}, f32[256]{0:T(256)S(1)}, /*index...) fusion(f32[256]{0:T(256)S(1)} %bitcast.3158, ...), kind=kLoop, calls=%fused_computation.230.clone.1 | loop fusion | flops 16384 | bytes 66688 | tf_op jit(solution)/shard_map/while/body/eval_jaxpr/sub | solution.py:45
  287.2 20.2 %multiply_subtract_fusion.253 = (f32[256]{0:T(256)S(1)}, f32[256]{0:T(256)S(1)}, f32[256]{0:T(256)S(1)}, f32[256]{0:T(256)S(1)}, f32[256]{0:T(256)S(1)}, /*index...) fusion(f32[256]{0:T(256)S(1)} %bitcast.3158, ...), kind=kLoop, calls=%fused_computation.230.clone.1 | loop fusion | flops 16384 | bytes 66688 | tf_op jit(solution)/shard_map/while/body/eval_jaxpr/sub | solution.py:45
  309.2 20.2 %multiply_subtract_fusion.253 = (f32[256]{0:T(256)S(1)}, f32[256]{0:T(256)S(1)}, f32[256]{0:T(256)S(1)}, f32[256]{0:T(256)S(1)}, f32[256]{0:T(256)S(1)}, /*index...) fusion(f32[256]{0:T(256)S(1)} %bitcast.3158, ...), kind=kLoop, calls=%fused_computation.230.clone.1 | loop fusion | flops 16384 | bytes 66688 | tf_op jit(solution)/shard_map/while/body/eval_jaxpr/sub | solution.py:45
  329.4 19.3 %multiply_subtract_fusion.66 = (f32[256]{0:T(256)S(1)}, f32[256]{0:T(256)S(1)}, f32[256]{0:T(256)S(1)}, f32[256]{0:T(256)S(1)}, f32[256]{0:T(256)S(1)}, /*index=...) fusion(f32[256]{0:T(256)S(1)} %bitcast.3585, ...), kind=kLoop, calls=%fused_computation.598 | loop fusion | flops 15872 | bytes 64636 | tf_op jit(solution)/shard_map/eval_jaxpr/sub | solution.py:45
  351.1 152.3 %while.97 = (s32[]{:T(128)}, f32[256]{0:T(256)S(1)}, f32[7,32,256]{2,1,0:T(8,128)S(1)}, f32[7,32,256]{2,1,0:T(8,128)S(1)}, f32[7,32]{1,0:T(8,128)S(1)}, /*index=...) while((s32[]{:T(128)}, f32[256]{0:T(256)S(1)}, ...), condition=%wide.region_3.4_spmd, body=%wide.region_2.3_spmd.sunk | while | flops 16418 | bytes 266721 | solution.py:45
  352.8 20.0 %multiply_subtract_fusion.252 = (f32[256]{0:T(256)S(1)}, f32[256]{0:T(256)S(1)}, f32[256]{0:T(256)S(1)}, f32[256]{0:T(256)S(1)}, f32[256]{0:T(256)S(1)}, /*index...) fusion(f32[256]{0:T(256)S(1)} %bitcast.3176, ...), kind=kLoop, calls=%fused_computation.99.clone.1 | loop fusion | flops 16384 | bytes 66688 | tf_op jit(solution)/shard_map/while/body/eval_jaxpr/sub | solution.py:45
  374.5 20.0 %multiply_subtract_fusion.252 = (f32[256]{0:T(256)S(1)}, f32[256]{0:T(256)S(1)}, f32[256]{0:T(256)S(1)}, f32[256]{0:T(256)S(1)}, f32[256]{0:T(256)S(1)}, /*index...) fusion(f32[256]{0:T(256)S(1)} %bitcast.3176, ...), kind=kLoop, calls=%fused_computation.99.clone.1 | loop fusion | flops 16384 | bytes 66688 | tf_op jit(solution)/shard_map/while/body/eval_jaxpr/sub | solution.py:45
  396.3 20.0 %multiply_subtract_fusion.252 = (f32[256]{0:T(256)S(1)}, f32[256]{0:T(256)S(1)}, f32[256]{0:T(256)S(1)}, f32[256]{0:T(256)S(1)}, f32[256]{0:T(256)S(1)}, /*index...) fusion(f32[256]{0:T(256)S(1)} %bitcast.3176, ...), kind=kLoop, calls=%fused_computation.99.clone.1 | loop fusion | flops 16384 | bytes 66688 | tf_op jit(solution)/shard_map/while/body/eval_jaxpr/sub | solution.py:45
  418.0 20.0 %multiply_subtract_fusion.252 = (f32[256]{0:T(256)S(1)}, f32[256]{0:T(256)S(1)}, f32[256]{0:T(256)S(1)}, f32[256]{0:T(256)S(1)}, f32[256]{0:T(256)S(1)}, /*index...) fusion(f32[256]{0:T(256)S(1)} %bitcast.3176, ...), kind=kLoop, calls=%fused_computation.99.clone.1 | loop fusion | flops 16384 | bytes 66688 | tf_op jit(solution)/shard_map/while/body/eval_jaxpr/sub | solution.py:45
  439.8 20.0 %multiply_subtract_fusion.252 = (f32[256]{0:T(256)S(1)}, f32[256]{0:T(256)S(1)}, f32[256]{0:T(256)S(1)}, f32[256]{0:T(256)S(1)}, f32[256]{0:T(256)S(1)}, /*index...) fusion(f32[256]{0:T(256)S(1)} %bitcast.3176, ...), kind=kLoop, calls=%fused_computation.99.clone.1 | loop fusion | flops 16384 | bytes 66688 | tf_op jit(solution)/shard_map/while/body/eval_jaxpr/sub | solution.py:45
  461.5 20.0 %multiply_subtract_fusion.252 = (f32[256]{0:T(256)S(1)}, f32[256]{0:T(256)S(1)}, f32[256]{0:T(256)S(1)}, f32[256]{0:T(256)S(1)}, f32[256]{0:T(256)S(1)}, /*index...) fusion(f32[256]{0:T(256)S(1)} %bitcast.3176, ...), kind=kLoop, calls=%fused_computation.99.clone.1 | loop fusion | flops 16384 | bytes 66688 | tf_op jit(solution)/shard_map/while/body/eval_jaxpr/sub | solution.py:45
  483.3 20.0 %multiply_subtract_fusion.252 = (f32[256]{0:T(256)S(1)}, f32[256]{0:T(256)S(1)}, f32[256]{0:T(256)S(1)}, f32[256]{0:T(256)S(1)}, f32[256]{0:T(256)S(1)}, /*index...) fusion(f32[256]{0:T(256)S(1)} %bitcast.3176, ...), kind=kLoop, calls=%fused_computation.99.clone.1 | loop fusion | flops 16384 | bytes 66688 | tf_op jit(solution)/shard_map/while/body/eval_jaxpr/sub | solution.py:45
  536.9 22.9 %reduce.12 = f32[4096,3,8]{2,1,0:T(4,128)} reduce(f32[4096,3,1,8]{3,2,1,0:T(1,128)} %bitcast.2960, f32[]{:T(128)} %broadcast.790), dimensions={2}, to_apply=%bitcast.1784.reduce_sub_computation | reduce | bytes 786436
  619.7 19.3 %multiply_subtract_fusion.97 = (f32[256]{0:T(256)S(1)}, f32[256]{0:T(256)S(1)}, f32[256]{0:T(256)S(1)}, f32[256]{0:T(256)S(1)}, f32[256]{0:T(256)S(1)}, /*index=...) fusion(f32[256]{0:T(256)S(1)} %bitcast.3554, ...), kind=kLoop, calls=%fused_computation.660 | loop fusion | flops 15872 | bytes 64636 | tf_op jit(solution)/shard_map/eval_jaxpr/sub | solution.py:45
  (477 shorter events, 237.1 us)
Async XLA Ops:
  2.0 514.9 %all-to-all-start = ((f32[3,256,1,128]{3,2,0,1:T(1,128)}), f32[3,256,1,128]{3,2,0,1:T(1,128)S(1)}, u32[]{:S(2)}, u32[]{:S(2)}) async-start(f32[3,256,1,128]{3,2,0,1:T(1,128)} %copy.113), calls=%async_computation | async-start | bytes 786432 | tf_op jit(solution)/shard_map/all_to_all | solution.py:147
  14.8 489.3 %collective-permute-start = (f32[6,3,1,128]{3,1,0,2:T(4,128)S(1)}, f32[6,3,1,128]{3,1,0,2:T(4,128)S(1)}, u32[]{:S(2)}, u32[]{:S(2)}) collective-permute-start(f32[6,3,1,128]{3,1,0,2:T(4,128)S(1)} %get-tuple-element.1127), channel_id=1, source_target_pairs={{32,0},{64,32},{96,64},{128,96},{160,128},{192,160},{224,192},{256... | collective-permute-start | bytes 27656 | tf_op jit(solution)/shard_map/ppermute | solution.py:22
  24.4 479.8 %collective-permute-start.1 = (f32[6,3,1,128]{3,1,0,2:T(4,128)S(1)}, f32[6,3,1,128]{3,1,0,2:T(4,128)S(1)}, u32[]{:S(2)}, u32[]{:S(2)}) collective-permute-start(f32[6,3,1,128]{3,1,0,2:T(4,128)S(1)} %get-tuple-element.1128), channel_id=1, source_target_pairs={{0,32},{32,64},{64,96},{96,128},{128,160},{160,192},{192,224},{224... | collective-permute-start | bytes 27656 | tf_op jit(solution)/shard_map/ppermute | solution.py:19
  32.2 100.7 %copy-start.8 = (f32[3,32,128]{2,1,0:T(8,128)}, f32[3,32,128]{2,1,0:T(8,128)S(1)}, u32[]{:S(2)}) copy-start(f32[3,32,128]{2,1,0:T(8,128)S(1)} %get-tuple-element.434) | copy-start | bytes 147460
  350.7 153.5 %copy-start = (f32[3,256,1,128]{3,2,1,0:T(1,128)S(1)}, f32[3,256,1,128]{3,2,1,0:T(1,128)}, u32[]{:S(2)}) copy-start(f32[3,256,1,128]{3,2,1,0:T(1,128)} %param.13) | copy-start | bytes 1179652
  505.4 6.7 %collective-permute-start.2 = (f32[6,1,1,128]{3,1,0,2:T(1,128)S(1)}, f32[6,1,1,128]{3,1,0,2:T(1,128)S(1)}, u32[]{:S(2)}, u32[]{:S(2)}) collective-permute-start(f32[6,1,1,128]{3,1,0,2:T(1,128)S(1)} %slice.4306), channel_id=1, source_target_pairs={{0,32},{32,64},{64,96},{96,128},{128,160},{160,192},{192,224},{224... | collective-permute-start | bytes 9224 | tf_op jit(solution)/shard_map/ppermute | solution.py:19
  512.7 63.5 %collective-permute-start.3 = (f32[6,1,1,128]{3,1,0,2:T(1,128)}, f32[6,1,1,128]{3,1,0,2:T(1,128)}, u32[]{:S(2)}, u32[]{:S(2)}) collective-permute-start(f32[6,1,1,128]{3,1,0,2:T(1,128)} %get-tuple-element.1124), channel_id=1, source_target_pairs={{32,0},{64,32},{96,64},{128,96},{160,128},{192,160},{224,192},{256... | collective-permute-start | bytes 9224 | tf_op jit(solution)/shard_map/ppermute | solution.py:22
  568.8 16.2 %all-to-all-start.1 = ((f32[32,1,3072]{2,1,0:T(1,128)}), f32[32,1,3072]{2,1,0:T(1,128)S(1)}, u32[]{:S(2)}, u32[]{:S(2)}) async-start(f32[32,1,3072]{2,1,0:T(1,128)} %reshape.854), calls=%async_computation.1 | async-start | bytes 786432 | tf_op jit(solution)/shard_map/all_to_all | solution.py:152
  599.4 20.0 %copy-start.12 = (f32[1,256]{1,0:T(1,128)S(1)}, f32[1,256]{1,0:T(1,128)}, u32[]{:S(2)}) copy-start(f32[1,256]{1,0:T(1,128)} %get-tuple-element.1191) | copy-start | bytes 3076
  599.4 20.0 %copy-start.13 = (f32[1,256]{1,0:T(1,128)S(1)}, f32[1,256]{1,0:T(1,128)}, u32[]{:S(2)}) copy-start(f32[1,256]{1,0:T(1,128)} %get-tuple-element.1192) | copy-start | bytes 3076
  599.4 20.0 %copy-start.14 = (f32[1,256]{1,0:T(1,128)S(1)}, f32[1,256]{1,0:T(1,128)}, u32[]{:S(2)}) copy-start(f32[1,256]{1,0:T(1,128)} %get-tuple-element.1193) | copy-start | bytes 3076
  599.4 20.0 %copy-start.15 = (f32[1,256]{1,0:T(1,128)S(1)}, f32[1,256]{1,0:T(1,128)}, u32[]{:S(2)}) copy-start(f32[1,256]{1,0:T(1,128)} %get-tuple-element.1194) | copy-start | bytes 3076
  599.5 20.0 %copy-start.16 = (f32[1,256]{1,0:T(1,128)S(1)}, f32[1,256]{1,0:T(1,128)}, u32[]{:S(2)}) copy-start(f32[1,256]{1,0:T(1,128)} %get-tuple-element.1195) | copy-start | bytes 3076
  599.5 20.0 %copy-start.17 = (f32[1,256]{1,0:T(1,128)S(1)}, f32[1,256]{1,0:T(1,128)}, u32[]{:S(2)}) copy-start(f32[1,256]{1,0:T(1,128)} %get-tuple-element.1196) | copy-start | bytes 3076
  599.5 20.0 %copy-start.18 = (f32[1,256]{1,0:T(1,128)S(1)}, f32[1,256]{1,0:T(1,128)}, u32[]{:S(2)}) copy-start(f32[1,256]{1,0:T(1,128)} %get-tuple-element.1197) | copy-start | bytes 3076
  599.5 20.0 %copy-start.19 = (f32[1,256]{1,0:T(1,128)S(1)}, f32[1,256]{1,0:T(1,128)}, u32[]{:S(2)}) copy-start(f32[1,256]{1,0:T(1,128)} %get-tuple-element.1198) | copy-start | bytes 3076
  599.5 20.0 %copy-start.20 = (f32[1,256]{1,0:T(1,128)S(1)}, f32[1,256]{1,0:T(1,128)}, u32[]{:S(2)}) copy-start(f32[1,256]{1,0:T(1,128)} %get-tuple-element.1199) | copy-start | bytes 3076
  599.5 20.0 %copy-start.21 = (f32[1,256]{1,0:T(1,128)S(1)}, f32[1,256]{1,0:T(1,128)}, u32[]{:S(2)}) copy-start(f32[1,256]{1,0:T(1,128)} %get-tuple-element.1169) | copy-start | bytes 3076
  599.5 20.0 %copy-start.22 = (f32[1,256]{1,0:T(1,128)S(1)}, f32[1,256]{1,0:T(1,128)}, u32[]{:S(2)}) copy-start(f32[1,256]{1,0:T(1,128)} %get-tuple-element.1170) | copy-start | bytes 3076
  599.7 39.4 %copy-start.5 = (f32[7,32,256]{2,1,0:T(8,128)S(1)}, f32[7,32,256]{2,1,0:T(8,128)}, u32[]{:S(2)}) copy-start(f32[7,32,256]{2,1,0:T(8,128)} %copy-done.4) | copy-start | bytes 688132
  612.3 26.8 %collective-permute-start.5 = (f32[3,3,1,128]{3,1,0,2:T(4,128)S(1)}, f32[3,3,1,128]{3,1,0,2:T(4,128)S(1)}, u32[]{:S(2)}, u32[]{:S(2)}) collective-permute-start(f32[3,3,1,128]{3,1,0,2:T(4,128)S(1)} %get-tuple-element.1134), channel_id=1, source_target_pairs={{0,32},{32,64},{64,96},{96,128},{128,160},{160,192},{192,224},{224... | collective-permute-start | bytes 13832 | tf_op jit(solution)/shard_map/ppermute | solution.py:19
  614.3 24.9 %collective-permute-start.4 = (f32[3,3,1,128]{3,1,0,2:T(4,128)S(1)}, f32[3,3,1,128]{3,1,0,2:T(4,128)S(1)}, u32[]{:S(2)}, u32[]{:S(2)}) collective-permute-start(f32[3,3,1,128]{3,1,0,2:T(4,128)S(1)} %get-tuple-element.1133), channel_id=1, source_target_pairs={{32,0},{64,32},{96,64},{128,96},{160,128},{192,160},{224,192},{256... | collective-permute-start | bytes 13832 | tf_op jit(solution)/shard_map/ppermute | solution.py:22
  640.1 6.7 %collective-permute-start.6 = (f32[3,1,1,128]{3,1,0,2:T(1,128)S(1)}, f32[3,1,1,128]{3,1,0,2:T(1,128)S(1)}, u32[]{:S(2)}, u32[]{:S(2)}) collective-permute-start(f32[3,1,1,128]{3,1,0,2:T(1,128)S(1)} %slice.4403), channel_id=1, source_target_pairs={{0,32},{32,64},{64,96},{96,128},{128,160},{160,192},{192,224},{224... | collective-permute-start | bytes 4616 | tf_op jit(solution)/shard_map/ppermute | solution.py:19
  646.8 5.5 collective-permute-start.7
  (26 other events, 455.9 us)
where the time goes:
time: 661 us; the launch traced here: 653 us
  other arithmetic  457 us (69%)
  local copies, waits for them, and re-layouts  97.7 us (15%)
  starting transfers between devices  46.2 us (7%)
  loops' own time  25.7 us (4%)
  waiting for transfers between devices  14.1 us (2%)
  between operations  8.93 us (1%)
    sub x19, other arithmetic, tables(): lax.linalg.tridiagonal_solve(lower_diag, main_diag, upper_diag, identity)  379 us
    broadcast_in_dim x17, other arithmetic, tables(): lax.linalg.tridiagonal_solve(lower_diag, main_diag, upper_diag, identity)  40.6 us
    slice x110, local copies, waits for them, and re-layouts, tables(): lax.linalg.tridiagonal_solve(lower_diag, main_diag, upper_diag, identity)  35.7 us
    another operation x6, loops' own time, tables(): lax.linalg.tridiagonal_solve(lower_diag, main_diag, upper_diag, identity)  25.7 us
    unnamed x89, local copies, waits for them, and re-layouts  25.6 us
    unnamed x1, other arithmetic  22.9 us
    ppermute x4, starting transfers between devices, with_halo(): lax.ppermute(lax.slice_in_dim(block, 0, width, axis=dim), axis, backward)  21.7 us
  transfers between devices with their start and end apart: 10, of which 4 were waited for; matrix products, arithmetic and copies ran while one was open for 81% of the time, Pallas kernels for 0%

commit v1 on v0

--- a/solution.py
+++ b/solution.py
@@ -8,6 +8,13 @@
 COEF_B = 1.0 / 9.0
 ALPHA_F = 0.49
 block_len = 128
+
+
+def swap_blocks(shard, mesh_axis, split, join):
+    devices = lax.axis_size(mesh_axis)
+    blocks = jnp.stack(jnp.split(shard, devices, axis=split), axis=0)
+    blocks = lax.all_to_all(blocks, mesh_axis, split_axis=0, concat_axis=0)
+    return jnp.concatenate(blocks, axis=join)
 
 
 def with_halo(block, sides, width):
@@ -149,7 +156,7 @@
     fields = jnp.concatenate([pencil, along_z * pencil], axis=0)
     slopes = solve_blocks(slope_rhs(wrap_pad(fields, 3), fields.shape[3], 3), slope_z)
     local_terms = slopes[3:] + along_z * slopes[:3]
-    return lax.all_to_all(local_terms, "gz", split_axis=3, concat_axis=1, tiled=True)
+    return swap_blocks(local_terms, "gz", 3, 1)
 
 
 def per_device(velocity):

time: 661 us -> 624 us (0.944)
  local copies, waits for them, and re-layouts: 97.7 us -> 72.8 us
  other arithmetic: 457 us -> 447 us
    unnamed x1 -> x0, other arithmetic: 22.9 us -> none
    all_to_all x1 -> x0, local copies, waits for them, and re-layouts: 12.3 us -> none  [z_part(): lax.all_to_all(local_terms, 'gz', split_axis=3, concat_axis=1, tiled=True)]
    add x1 -> x0, local copies, waits for them, and re-layouts: 10.4 us -> none  [z_part(): local_terms = slopes[3:] + along_z * slopes[:3]]
    add x0 -> x1, other arithmetic: none -> 6.65 us  [slope_rhs(): rhs + COEF_B * 0.25 * (offset_slice(extended, 2, length, direction, base)...]
    unnamed x89 -> x73, local copies, waits for them, and re-layouts: 25.6 us -> 20.7 us
  transfers between devices with their start and end apart: 10 -> 10, of which waited for: 4 -> 4; matrix products, arithmetic and copies ran while one was open for 81% -> 84% of each run, Pallas kernels for 0% -> 0%
where the time goes in v1:
time: 624 us; the launch traced here: 617 us
  other arithmetic  447 us (72%)
  local copies, waits for them, and re-layouts  72.8 us (12%)
  starting transfers between devices  45.7 us (7%)
  loops' own time  25.8 us (4%)
  waiting for transfers between devices  13.3 us (2%)
  between operations  8.81 us (1%)
    sub x19, other arithmetic, tables(): lax.linalg.tridiagonal_solve(lower_diag, main_diag, upper_diag, identity)  383 us
    broadcast_in_dim x17, other arithmetic, tables(): lax.linalg.tridiagonal_solve(lower_diag, main_diag, upper_diag, identity)  40.6 us
    slice x110, local copies, waits for them, and re-layouts, tables(): lax.linalg.tridiagonal_solve(lower_diag, main_diag, upper_diag, identity)  36.2 us
    another operation x6, loops' own time, tables(): lax.linalg.tridiagonal_solve(lower_diag, main_diag, upper_diag, identity)  25.8 us
    ppermute x4, starting transfers between devices, with_halo(): lax.ppermute(lax.slice_in_dim(block, 0, width, axis=dim), axis, backward)  20.9 us
    unnamed x73, local copies, waits for them, and re-layouts  20.7 us
  transfers between devices with their start and end apart: 10, of which 4 were waited for; matrix products, arithmetic and copies ran while one was open for 84% of the time, Pallas kernels for 0%

profile of v1, /device:TPU:2, one launch (start us, length us, event | category | flops | bytes accessed | tf_op | source)
XLA Modules:
  0.0 617.3 jit_solution(1798751698362468421)
XLA Ops:
  25.9 14.9 %while.96 = (s32[]{:T(128)}, f32[]{:T(128)}, f32[256]{0:T(256)S(1)}, f32[7,32]{1,0:T(8,128)S(1)}, f32[7,32,256]{2,1,0:T(8,128)S(1)}, /*index=5*/f32[7,32,256]{2,...) while((s32[]{:T(128)}, f32[]{:T(128)}, ...), condition=%wide.region_1.2_spmd, body=%wide.region_0.1_spmd.sunk | while | flops 24705 | bytes 267869 | solution.py:52
  49.6 14.9 %while.98 = (s32[]{:T(128)}, f32[]{:T(128)}, f32[256]{0:T(256)S(1)}, f32[7,32]{1,0:T(8,128)S(1)}, f32[7,32,256]{2,1,0:T(8,128)S(1)}, /*index=5*/f32[7,32,256]{2,...) while((s32[]{:T(128)}, f32[]{:T(128)}, ...), condition=%wide.region_5.6_spmd, body=%wide.region_4.5_spmd.sunk | while | flops 24705 | bytes 267869 | solution.py:52
  68.1 154.3 %while.97 = (s32[]{:T(128)}, f32[256]{0:T(256)S(1)}, f32[7,32,256]{2,1,0:T(8,128)S(1)}, f32[7,32,256]{2,1,0:T(8,128)S(1)}, f32[7,32]{1,0:T(8,128)S(1)}, /*index=...) while((s32[]{:T(128)}, f32[256]{0:T(256)S(1)}, ...), condition=%wide.region_3.4_spmd, body=%wide.region_2.3_spmd.sunk | while | flops 16418 | bytes 266713 | solution.py:52
  69.8 20.2 %multiply_subtract_fusion.252 = (f32[256]{0:T(256)S(1)}, f32[256]{0:T(256)S(1)}, f32[256]{0:T(256)S(1)}, f32[256]{0:T(256)S(1)}, f32[256]{0:T(256)S(1)}, /*index...) fusion(f32[256]{0:T(256)S(1)} %bitcast.3249, ...), kind=kLoop, calls=%fused_computation.99.clone.1 | loop fusion | flops 16384 | bytes 66688 | tf_op jit(solution)/shard_map/while/body/eval_jaxpr/sub | solution.py:52
  91.8 20.2 %multiply_subtract_fusion.252 = (f32[256]{0:T(256)S(1)}, f32[256]{0:T(256)S(1)}, f32[256]{0:T(256)S(1)}, f32[256]{0:T(256)S(1)}, f32[256]{0:T(256)S(1)}, /*index...) fusion(f32[256]{0:T(256)S(1)} %bitcast.3249, ...), kind=kLoop, calls=%fused_computation.99.clone.1 | loop fusion | flops 16384 | bytes 66688 | tf_op jit(solution)/shard_map/while/body/eval_jaxpr/sub | solution.py:52
  113.9 20.2 %multiply_subtract_fusion.252 = (f32[256]{0:T(256)S(1)}, f32[256]{0:T(256)S(1)}, f32[256]{0:T(256)S(1)}, f32[256]{0:T(256)S(1)}, f32[256]{0:T(256)S(1)}, /*index...) fusion(f32[256]{0:T(256)S(1)} %bitcast.3249, ...), kind=kLoop, calls=%fused_computation.99.clone.1 | loop fusion | flops 16384 | bytes 66688 | tf_op jit(solution)/shard_map/while/body/eval_jaxpr/sub | solution.py:52
  135.9 20.2 %multiply_subtract_fusion.252 = (f32[256]{0:T(256)S(1)}, f32[256]{0:T(256)S(1)}, f32[256]{0:T(256)S(1)}, f32[256]{0:T(256)S(1)}, f32[256]{0:T(256)S(1)}, /*index...) fusion(f32[256]{0:T(256)S(1)} %bitcast.3249, ...), kind=kLoop, calls=%fused_computation.99.clone.1 | loop fusion | flops 16384 | bytes 66688 | tf_op jit(solution)/shard_map/while/body/eval_jaxpr/sub | solution.py:52
  158.0 20.2 %multiply_subtract_fusion.252 = (f32[256]{0:T(256)S(1)}, f32[256]{0:T(256)S(1)}, f32[256]{0:T(256)S(1)}, f32[256]{0:T(256)S(1)}, f32[256]{0:T(256)S(1)}, /*index...) fusion(f32[256]{0:T(256)S(1)} %bitcast.3249, ...), kind=kLoop, calls=%fused_computation.99.clone.1 | loop fusion | flops 16384 | bytes 66688 | tf_op jit(solution)/shard_map/while/body/eval_jaxpr/sub | solution.py:52
  180.0 20.2 %multiply_subtract_fusion.252 = (f32[256]{0:T(256)S(1)}, f32[256]{0:T(256)S(1)}, f32[256]{0:T(256)S(1)}, f32[256]{0:T(256)S(1)}, f32[256]{0:T(256)S(1)}, /*index...) fusion(f32[256]{0:T(256)S(1)} %bitcast.3249, ...), kind=kLoop, calls=%fused_computation.99.clone.1 | loop fusion | flops 16384 | bytes 66688 | tf_op jit(solution)/shard_map/while/body/eval_jaxpr/sub | solution.py:52
  202.0 20.2 %multiply_subtract_fusion.252 = (f32[256]{0:T(256)S(1)}, f32[256]{0:T(256)S(1)}, f32[256]{0:T(256)S(1)}, f32[256]{0:T(256)S(1)}, f32[256]{0:T(256)S(1)}, /*index...) fusion(f32[256]{0:T(256)S(1)} %bitcast.3249, ...), kind=kLoop, calls=%fused_computation.99.clone.1 | loop fusion | flops 16384 | bytes 66688 | tf_op jit(solution)/shard_map/while/body/eval_jaxpr/sub | solution.py:52
  224.2 65.4 %while.101 = (s32[]{:T(128)}, f32[128]{0:T(128)S(1)}, f32[3,32,128]{2,1,0:T(8,128)S(1)}, f32[3,32,128]{2,1,0:T(8,128)S(1)}, f32[3,32]{1,0:T(4,128)S(1)}, /*index...) while((s32[]{:T(128)}, f32[128]{0:T(128)S(1)}, ...), condition=%wide.region_11.12_spmd, body=%wide.region_10.11_spmd.sunk | while | flops 8226 | bytes 101333 | solution.py:52
  225.7 20.2 %fusion.492 = (f32[128]{0:T(128)S(1)}, f32[128]{0:T(128)S(1)}, f32[128]{0:T(128)S(1)}, f32[128]{0:T(128)S(1)}, f32[128]{0:T(128)S(1)}, /*index=5*/f32[128]{0:T(1...) fusion(f32[3,32,128]{2,1,0:T(8,128)S(1)} %get-tuple-element.283, ...), kind=kLoop, calls=%fused_computation.428.clone.1 | loop fusion | flops 8192 | bytes 33536 | tf_op jit(solution)/shard_map/while/body/eval_jaxpr/sub | solution.py:52
  247.5 20.2 %fusion.492 = (f32[128]{0:T(128)S(1)}, f32[128]{0:T(128)S(1)}, f32[128]{0:T(128)S(1)}, f32[128]{0:T(128)S(1)}, f32[128]{0:T(128)S(1)}, /*index=5*/f32[128]{0:T(1...) fusion(f32[3,32,128]{2,1,0:T(8,128)S(1)} %get-tuple-element.283, ...), kind=kLoop, calls=%fused_computation.428.clone.1 | loop fusion | flops 8192 | bytes 33536 | tf_op jit(solution)/shard_map/while/body/eval_jaxpr/sub | solution.py:52
  269.3 20.2 %fusion.492 = (f32[128]{0:T(128)S(1)}, f32[128]{0:T(128)S(1)}, f32[128]{0:T(128)S(1)}, f32[128]{0:T(128)S(1)}, f32[128]{0:T(128)S(1)}, /*index=5*/f32[128]{0:T(1...) fusion(f32[3,32,128]{2,1,0:T(8,128)S(1)} %get-tuple-element.283, ...), kind=kLoop, calls=%fused_computation.428.clone.1 | loop fusion | flops 8192 | bytes 33536 | tf_op jit(solution)/shard_map/while/body/eval_jaxpr/sub | solution.py:52
  333.0 153.8 %while.99 = (s32[]{:T(128)}, f32[256]{0:T(256)S(1)}, f32[7,32,256]{2,1,0:T(8,128)S(1)}, f32[7,32,256]{2,1,0:T(8,128)S(1)}, f32[7,32]{1,0:T(8,128)S(1)}, /*index=...) while((s32[]{:T(128)}, f32[256]{0:T(256)S(1)}, ...), condition=%wide.region_7.8_spmd, body=%wide.region_6.7_spmd.sunk | while | flops 16418 | bytes 266713 | solution.py:52
  334.7 20.2 %multiply_subtract_fusion.253 = (f32[256]{0:T(256)S(1)}, f32[256]{0:T(256)S(1)}, f32[256]{0:T(256)S(1)}, f32[256]{0:T(256)S(1)}, f32[256]{0:T(256)S(1)}, /*index...) fusion(f32[256]{0:T(256)S(1)} %bitcast.3267, ...), kind=kLoop, calls=%fused_computation.230.clone.1 | loop fusion | flops 16384 | bytes 66688 | tf_op jit(solution)/shard_map/while/body/eval_jaxpr/sub | solution.py:52
  356.6 20.2 %multiply_subtract_fusion.253 = (f32[256]{0:T(256)S(1)}, f32[256]{0:T(256)S(1)}, f32[256]{0:T(256)S(1)}, f32[256]{0:T(256)S(1)}, f32[256]{0:T(256)S(1)}, /*index...) fusion(f32[256]{0:T(256)S(1)} %bitcast.3267, ...), kind=kLoop, calls=%fused_computation.230.clone.1 | loop fusion | flops 16384 | bytes 66688 | tf_op jit(solution)/shard_map/while/body/eval_jaxpr/sub | solution.py:52
  378.6 20.2 %multiply_subtract_fusion.253 = (f32[256]{0:T(256)S(1)}, f32[256]{0:T(256)S(1)}, f32[256]{0:T(256)S(1)}, f32[256]{0:T(256)S(1)}, f32[256]{0:T(256)S(1)}, /*index...) fusion(f32[256]{0:T(256)S(1)} %bitcast.3267, ...), kind=kLoop, calls=%fused_computation.230.clone.1 | loop fusion | flops 16384 | bytes 66688 | tf_op jit(solution)/shard_map/while/body/eval_jaxpr/sub | solution.py:52
  400.6 20.2 %multiply_subtract_fusion.253 = (f32[256]{0:T(256)S(1)}, f32[256]{0:T(256)S(1)}, f32[256]{0:T(256)S(1)}, f32[256]{0:T(256)S(1)}, f32[256]{0:T(256)S(1)}, /*index...) fusion(f32[256]{0:T(256)S(1)} %bitcast.3267, ...), kind=kLoop, calls=%fused_computation.230.clone.1 | loop fusion | flops 16384 | bytes 66688 | tf_op jit(solution)/shard_map/while/body/eval_jaxpr/sub | solution.py:52
  422.5 20.2 %multiply_subtract_fusion.253 = (f32[256]{0:T(256)S(1)}, f32[256]{0:T(256)S(1)}, f32[256]{0:T(256)S(1)}, f32[256]{0:T(256)S(1)}, f32[256]{0:T(256)S(1)}, /*index...) fusion(f32[256]{0:T(256)S(1)} %bitcast.3267, ...), kind=kLoop, calls=%fused_computation.230.clone.1 | loop fusion | flops 16384 | bytes 66688 | tf_op jit(solution)/shard_map/while/body/eval_jaxpr/sub | solution.py:52
  444.5 20.2 %multiply_subtract_fusion.253 = (f32[256]{0:T(256)S(1)}, f32[256]{0:T(256)S(1)}, f32[256]{0:T(256)S(1)}, f32[256]{0:T(256)S(1)}, f32[256]{0:T(256)S(1)}, /*index...) fusion(f32[256]{0:T(256)S(1)} %bitcast.3267, ...), kind=kLoop, calls=%fused_computation.230.clone.1 | loop fusion | flops 16384 | bytes 66688 | tf_op jit(solution)/shard_map/while/body/eval_jaxpr/sub | solution.py:52
  466.5 20.2 %multiply_subtract_fusion.253 = (f32[256]{0:T(256)S(1)}, f32[256]{0:T(256)S(1)}, f32[256]{0:T(256)S(1)}, f32[256]{0:T(256)S(1)}, f32[256]{0:T(256)S(1)}, /*index...) fusion(f32[256]{0:T(256)S(1)} %bitcast.3267, ...), kind=kLoop, calls=%fused_computation.230.clone.1 | loop fusion | flops 16384 | bytes 66688 | tf_op jit(solution)/shard_map/while/body/eval_jaxpr/sub | solution.py:52
  486.8 19.4 %multiply_subtract_fusion.66 = (f32[256]{0:T(256)S(1)}, f32[256]{0:T(256)S(1)}, f32[256]{0:T(256)S(1)}, f32[256]{0:T(256)S(1)}, f32[256]{0:T(256)S(1)}, /*index=...) fusion(f32[256]{0:T(256)S(1)} %bitcast.3727, ...), kind=kLoop, calls=%fused_computation.627 | loop fusion | flops 15872 | bytes 64636 | tf_op jit(solution)/shard_map/eval_jaxpr/sub | solution.py:52
  582.8 20.3 %multiply_subtract_fusion.97 = (f32[256]{0:T(256)S(1)}, f32[256]{0:T(256)S(1)}, f32[256]{0:T(256)S(1)}, f32[256]{0:T(256)S(1)}, f32[256]{0:T(256)S(1)}, /*index=...) fusion(f32[256]{0:T(256)} %bitcast.3696, ...), kind=kLoop, calls=%fused_computation.689 | loop fusion | flops 15872 | bytes 64636 | tf_op jit(solution)/shard_map/eval_jaxpr/sub | solution.py:52
  (460 shorter events, 205.5 us)
Async XLA Ops:
  2.0 518.0 %all-to-all-start = ((f32[3,256,1,128]{3,2,0,1:T(1,128)}), f32[3,256,1,128]{3,2,0,1:T(1,128)S(1)}, u32[]{:S(2)}, u32[]{:S(2)}) async-start(f32[3,256,1,128]{3,2,0,1:T(1,128)} %copy.150), calls=%async_computation | async-start | bytes 786432 | tf_op jit(solution)/shard_map/all_to_all | solution.py:154
  14.2 493.0 %collective-permute-start = (f32[6,3,1,128]{3,1,0,2:T(4,128)S(1)}, f32[6,3,1,128]{3,1,0,2:T(4,128)S(1)}, u32[]{:S(2)}, u32[]{:S(2)}) collective-permute-start(f32[6,3,1,128]{3,1,0,2:T(4,128)S(1)} %get-tuple-element.1127), channel_id=1, source_target_pairs={{32,0},{64,32},{96,64},{128,96},{160,128},{192,160},{224,192},{256... | collective-permute-start | bytes 27656 | tf_op jit(solution)/shard_map/ppermute | solution.py:29
  23.8 483.5 %collective-permute-start.1 = (f32[6,3,1,128]{3,1,0,2:T(4,128)S(1)}, f32[6,3,1,128]{3,1,0,2:T(4,128)S(1)}, u32[]{:S(2)}, u32[]{:S(2)}) collective-permute-start(f32[6,3,1,128]{3,1,0,2:T(4,128)S(1)} %get-tuple-element.1128), channel_id=1, source_target_pairs={{0,32},{32,64},{64,96},{96,128},{128,160},{160,192},{192,224},{224... | collective-permute-start | bytes 27656 | tf_op jit(solution)/shard_map/ppermute | solution.py:26
  48.1 241.6 %copy-start.7 = (f32[3,32,128]{2,1,0:T(8,128)}, f32[3,32,128]{2,1,0:T(8,128)S(1)}, u32[]{:S(2)}) copy-start(f32[3,32,128]{2,1,0:T(8,128)S(1)} %get-tuple-element.434) | copy-start | bytes 147460
  222.4 107.9 %copy-start.3 = (f32[7,32,256]{2,1,0:T(8,128)}, f32[7,32,256]{2,1,0:T(8,128)S(1)}, u32[]{:S(2)}) copy-start(f32[7,32,256]{2,1,0:T(8,128)S(1)} %get-tuple-element.427) | copy-start | bytes 688132
  333.0 174.3 %copy-start = (f32[3,256,1,128]{3,2,1,0:T(1,128)S(1)}, f32[3,256,1,128]{3,2,1,0:T(1,128)}, u32[]{:S(2)}) copy-start(f32[3,256,1,128]{3,2,1,0:T(1,128)} %param.13) | copy-start | bytes 1179652
  508.6 6.7 %collective-permute-start.2 = (f32[6,1,1,128]{3,1,0,2:T(1,128)S(1)}, f32[6,1,1,128]{3,1,0,2:T(1,128)S(1)}, u32[]{:S(2)}, u32[]{:S(2)}) collective-permute-start(f32[6,1,1,128]{3,1,0,2:T(1,128)S(1)} %slice.4306), channel_id=1, source_target_pairs={{0,32},{32,64},{64,96},{96,128},{128,160},{160,192},{192,224},{224... | collective-permute-start | bytes 9224 | tf_op jit(solution)/shard_map/ppermute | solution.py:26
  515.9 52.1 %collective-permute-start.3 = (f32[6,1,1,128]{3,1,0,2:T(1,128)}, f32[6,1,1,128]{3,1,0,2:T(1,128)}, u32[]{:S(2)}, u32[]{:S(2)}) collective-permute-start(f32[6,1,1,128]{3,1,0,2:T(1,128)} %get-tuple-element.1124), channel_id=1, source_target_pairs={{32,0},{64,32},{96,64},{128,96},{160,128},{192,160},{224,192},{256... | collective-permute-start | bytes 9224 | tf_op jit(solution)/shard_map/ppermute | solution.py:29
  539.0 29.0 %copy-start.6 = (f32[6,256,1,128]{3,1,0,2:T(8,128)S(1)}, f32[6,256,1,128]{3,1,0,2:T(8,128)}, u32[]{:S(2)}) copy-start(f32[6,256,1,128]{3,1,0,2:T(8,128)} %copy-done.5) | copy-start | bytes 2359300
  539.4 37.4 %copy-start.2 = (f32[1,256,1,128]{3,2,1,0:T(1,128)S(1)}, f32[1,256,1,128]{3,2,1,0:T(1,128)}, u32[]{:S(2)}) copy-start(f32[1,256,1,128]{3,2,1,0:T(1,128)} %copy-done.1) | copy-start | bytes 393220
  541.1 41.6 %copy-start.8 = (f32[1,256]{1,0:T(1,128)S(1)}, f32[1,256]{1,0:T(1,128)}, u32[]{:S(2)}) copy-start(f32[1,256]{1,0:T(1,128)} %get-tuple-element.1199) | copy-start | bytes 3076
  541.1 41.6 %copy-start.9 = (f32[1,256]{1,0:T(1,128)S(1)}, f32[1,256]{1,0:T(1,128)}, u32[]{:S(2)}) copy-start(f32[1,256]{1,0:T(1,128)} %get-tuple-element.1200) | copy-start | bytes 3076
  541.1 41.6 %copy-start.10 = (f32[1,256]{1,0:T(1,128)S(1)}, f32[1,256]{1,0:T(1,128)}, u32[]{:S(2)}) copy-start(f32[1,256]{1,0:T(1,128)} %get-tuple-element.1201) | copy-start | bytes 3076
  541.1 41.6 %copy-start.11 = (f32[1,256]{1,0:T(1,128)S(1)}, f32[1,256]{1,0:T(1,128)}, u32[]{:S(2)}) copy-start(f32[1,256]{1,0:T(1,128)} %get-tuple-element.1202) | copy-start | bytes 3076
  541.1 41.6 %copy-start.12 = (f32[1,256]{1,0:T(1,128)S(1)}, f32[1,256]{1,0:T(1,128)}, u32[]{:S(2)}) copy-start(f32[1,256]{1,0:T(1,128)} %get-tuple-element.1203) | copy-start | bytes 3076
  541.1 41.6 %copy-start.13 = (f32[1,256]{1,0:T(1,128)S(1)}, f32[1,256]{1,0:T(1,128)}, u32[]{:S(2)}) copy-start(f32[1,256]{1,0:T(1,128)} %get-tuple-element.1204) | copy-start | bytes 3076
  541.2 41.6 %copy-start.14 = (f32[1,256]{1,0:T(1,128)S(1)}, f32[1,256]{1,0:T(1,128)}, u32[]{:S(2)}) copy-start(f32[1,256]{1,0:T(1,128)} %get-tuple-element.1205) | copy-start | bytes 3076
  541.2 41.6 %copy-start.15 = (f32[1,256]{1,0:T(1,128)S(1)}, f32[1,256]{1,0:T(1,128)}, u32[]{:S(2)}) copy-start(f32[1,256]{1,0:T(1,128)} %get-tuple-element.1206) | copy-start | bytes 3076
  541.2 62.0 %copy-start.4 = (f32[7,32,256]{2,1,0:T(8,128)S(1)}, f32[7,32,256]{2,1,0:T(8,128)}, u32[]{:S(2)}) copy-start(f32[7,32,256]{2,1,0:T(8,128)} %copy-done.3) | copy-start | bytes 688132
  560.6 16.2 %all-to-all-start.1 = ((f32[32,3,8,1,128]{4,2,1,3,0:T(8,128)}), f32[32,3,8,1,128]{4,2,1,3,0:T(8,128)S(1)}, u32[]{:S(2)}, u32[]{:S(2)}) async-start(f32[32,3,8,1,128]{4,2,1,3,0:T(8,128)} %constant_dynamic-update-slice_fusion), calls=%async_computation.1 | async-start | bytes 786432 | tf_op jit(solution)/shard_map/all_to_all | solution.py:16
  576.9 26.4 %collective-permute-start.4 = (f32[3,3,1,128]{3,1,0,2:T(4,128)S(1)}, f32[3,3,1,128]{3,1,0,2:T(4,128)S(1)}, u32[]{:S(2)}, u32[]{:S(2)}) collective-permute-start(f32[3,3,1,128]{3,1,0,2:T(4,128)S(1)} %get-tuple-element.1133), channel_id=1, source_target_pairs={{32,0},{64,32},{96,64},{128,96},{160,128},{192,160},{224,192},{256... | collective-permute-start | bytes 13832 | tf_op jit(solution)/shard_map/ppermute | solution.py:29
  580.5 22.8 %collective-permute-start.5 = (f32[3,3,1,128]{3,1,0,2:T(4,128)S(1)}, f32[3,3,1,128]{3,1,0,2:T(4,128)S(1)}, u32[]{:S(2)}, u32[]{:S(2)}) collective-permute-start(f32[3,3,1,128]{3,1,0,2:T(4,128)S(1)} %get-tuple-element.1134), channel_id=1, source_target_pairs={{0,32},{32,64},{64,96},{96,128},{128,160},{160,192},{192,224},{224... | collective-permute-start | bytes 13832 | tf_op jit(solution)/shard_map/ppermute | solution.py:26
  604.2 6.7 %collective-permute-start.6 = (f32[3,1,1,128]{3,1,0,2:T(1,128)S(1)}, f32[3,1,1,128]{3,1,0,2:T(1,128)S(1)}, u32[]{:S(2)}, u32[]{:S(2)}) collective-permute-start(f32[3,1,1,128]{3,1,0,2:T(1,128)S(1)} %slice.4403), channel_id=1, source_target_pairs={{0,32},{32,64},{64,96},{96,128},{128,160},{160,192},{192,224},{224... | collective-permute-start | bytes 4616 | tf_op jit(solution)/shard_map/ppermute | solution.py:26
  610.9 5.5 collective-permute-start.7
  (4 other events, 32.8 us)
